TPU v7x, 32 devices: a whole 2x2x4 slice. The times are simulated.
32 devices in a mesh: section: 4 (over y, x), tp: 8 (over z, core).
Axes of the slice: x: 2, y: 2, z: 4, core: 2. Of those that a mesh axis runs over, the one named last changes fastest.
Arguments:
- inputs_now: bfloat16 [1536, 6144], P(('section', 'tp')), may hold values from -6 to 6
- cotangents: bfloat16 [1536, 6144], P(('section', 'tp')), may hold values from -6 to 6
- stashed: bfloat16 [3, 1536, 6144], P(None, ('section', 'tp')), may hold values from -6 to 6
- plan: int32 [4], replicated, may hold values from 0 to 2
- fwd_scores: bfloat16 [4, 48, 384, 384], P('section', 'tp'), may hold values from -9 to 300, as said below
- back_scores: bfloat16 [4, 48, 384, 384], P('section', 'tp'), may hold values from -9 to 300, as said below
- value_weight: bfloat16 [4, 6144, 6144], P('section', None, 'tp'), may hold values from -0.078125 to 0.078125
- out_weight: bfloat16 [4, 6144, 6144], P('section', 'tp'), may hold values from -0.21875 to 0.21875
Outputs:
- handed_on: bfloat16 [1536, 6144], P(('section', 'tp'))
- grad_back: bfloat16 [1536, 6144], P(('section', 'tp'))
- stash_next: bfloat16 [3, 1536, 6144], P(None, ('section', 'tp'))
- value_grad: bfloat16 [4, 6144, 6144], P('section', None, 'tp')
- out_grad: bfloat16 [4, 6144, 6144], P('section', 'tp')
Inputs may be any that keep to these rules, and one draw needn't show every extreme that they name: plan[s] names the slot, in the stash rows of section 3 - s, that holds section s's micro-batch for this tick's backward. `fwd_scores`: logits of keys later than the query are never read. `back_scores`: logits of keys later than the query are never read.
All inputs are finite; a program needn't handle non-finite values.
Results may differ from a plain program's by a relative error of at most 0.012.
Values may be sent and summed in bfloat16 or wider, within the bound.
A program may use at most 192 MiB of HBM per device.

v0:
```python
import jax
import jax.numpy as jnp
from jax import lax
from jax.sharding import PartitionSpec as P

HEAD = 128


eps = 1e-05


def passed_along(array, axis, by):
    size = lax.axis_size(axis)
    return lax.ppermute(array, axis, [(i, (i + by) % size) for i in range(size)])


def partner(value, axis, stride):
    mask = 2**stride
    pairs = [(source, source ^ mask) for source in range(lax.axis_size(axis))]
    return lax.ppermute(value, axis, pairs)


def normalize(layer_rows):
    average = jnp.mean(layer_rows, axis=-1, keepdims=True)
    centred = layer_rows - average
    inv_scale = lax.rsqrt(jnp.mean(centred * centred, axis=-1, keepdims=True) + eps)
    return (centred * inv_scale, inv_scale)


def causal_softmax(scores):
    logits = scores.astype(jnp.float32)
    rows = logits.shape[-1]
    causal = lax.broadcasted_iota(jnp.int32, (rows, rows), 0) >= lax.broadcasted_iota(
        jnp.int32, (rows, rows), 1
    )
    logits = jnp.where(causal, logits, -1e30)
    row_top = jnp.max(logits, axis=-1, keepdims=True)
    raised = jnp.where(causal, jnp.exp(logits - row_top), 0.0)
    return (raised / jnp.sum(raised, axis=-1, keepdims=True)).astype(jnp.bfloat16)


def mix_heads(weights, value_rows):
    rows = value_rows.shape[0]
    head_count = weights.shape[0]
    by_head = value_rows.reshape(rows, head_count, HEAD)
    mixed = jnp.einsum("hqk,khe->qhe", weights, by_head, preferred_element_type=jnp.float32)
    return mixed.reshape(rows, head_count * HEAD).astype(jnp.bfloat16)


def per_device(
    inputs_now, cotangents, stashed, plan, fwd_scores, back_scores, value_weight, out_weight
):
    tp_count = lax.axis_size("tp")
    sections = lax.axis_size("section")
    tp_index = lax.axis_index("tp")
    section_idx = lax.axis_index("section")
    mirror = sections - 1 - section_idx
    share_rows = inputs_now.shape[0]
    all_rows = share_rows * tp_count
    weight_in = value_weight[0]
    weight_out = out_weight[0]
    col_share = weight_in.shape[1]
    layer_rows = inputs_now.astype(jnp.float32)
    unit_rows, _ = normalize(layer_rows)
    normed = unit_rows.astype(jnp.bfloat16)
    values = jnp.dot(
        lax.all_gather(normed, "tp", axis=0, tiled=True),
        weight_in,
        preferred_element_type=jnp.float32,
    ).astype(jnp.bfloat16)
    context = mix_heads(causal_softmax(fwd_scores[0]), values)
    summed = lax.psum(
        jnp.dot(context, weight_out, preferred_element_type=jnp.float32).astype(jnp.bfloat16), "tp"
    ).astype(jnp.float32)
    branch = lax.dynamic_slice_in_dim(summed, tp_index * share_rows, share_rows, 0)
    layer_out = (layer_rows + branch).astype(jnp.bfloat16)
    handed_on = passed_along(layer_out, "section", 1)
    lookup = jnp.arange(sections, dtype=jnp.int32)
    owner_slot = jnp.sum(jnp.where(lookup == mirror, plan, 0))
    guest_rows = lax.dynamic_index_in_dim(stashed, owner_slot, 0, keepdims=False)
    outgoing = jnp.stack([guest_rows, inputs_now])
    incoming = outgoing
    for flip_bit in range(sections.bit_length() - 1):
        incoming = partner(incoming, "section", flip_bit)
    stored = incoming[0]
    arrived = incoming[1]
    stash_next = lax.dynamic_update_index_in_dim(stashed, arrived, owner_slot, 0)
    stash_unit, stash_scale = normalize(stored.astype(jnp.float32))
    stash_normed = stash_unit.astype(jnp.bfloat16)
    piece_norm = lax.all_gather(stash_normed, "tp", axis=0, tiled=True)
    piece_cot = lax.all_gather(cotangents, "tp", axis=0, tiled=True)
    rows_norm = piece_norm
    rows_cot = piece_cot
    piece_value = jnp.dot(piece_norm, weight_in, preferred_element_type=jnp.float32).astype(
        jnp.bfloat16
    )
    rows_value = piece_value
    piece_grad = jnp.einsum(
        "td,hd->th", piece_cot, weight_out, preferred_element_type=jnp.float32
    ).astype(jnp.bfloat16)
    rows_grad = piece_grad
    rows_norm, rows_cot, rows_value, rows_grad = (rows_norm, rows_cot, rows_value, rows_grad)
    back_probs = causal_softmax(back_scores[0])
    stash_context = mix_heads(back_probs, rows_value)
    grad_outw = jnp.einsum("th,td->hd", stash_context, rows_cot, preferred_element_type=jnp.float32)
    head_count = back_probs.shape[0]
    value_back = (
        jnp.einsum(
            "hqk,qhe->khe",
            back_probs,
            rows_grad.reshape(all_rows, head_count, HEAD),
            preferred_element_type=jnp.float32,
        )
        .reshape(all_rows, col_share)
        .astype(jnp.bfloat16)
    )
    grad_valw = jnp.einsum("td,th->dh", rows_norm, value_back, preferred_element_type=jnp.float32)
    summed_back = lax.psum(
        jnp.einsum("th,dh->td", value_back, weight_in, preferred_element_type=jnp.float32).astype(
            jnp.bfloat16
        ),
        "tp",
    ).astype(jnp.float32)
    norm_grad = lax.dynamic_slice_in_dim(summed_back, tp_index * share_rows, share_rows, 0)
    input_grad = cotangents.astype(jnp.float32) + stash_scale * (
        norm_grad
        - jnp.mean(norm_grad, axis=-1, keepdims=True)
        - stash_unit * jnp.mean(norm_grad * stash_unit, axis=-1, keepdims=True)
    )
    grad_back = passed_along(input_grad.astype(jnp.bfloat16), "section", -1)
    return (
        handed_on,
        grad_back,
        stash_next,
        grad_valw.astype(jnp.bfloat16)[None],
        grad_outw.astype(jnp.bfloat16)[None],
    )


def solution(mesh):
    return jax.shard_map(
        per_device,
        mesh=mesh,
        in_specs=(
            P(("section", "tp"), None),
            P(("section", "tp"), None),
            P(None, ("section", "tp"), None),
            P(),
            P("section", "tp", None, None),
            P("section", "tp", None, None),
            P("section", None, "tp"),
            P("section", "tp", None),
        ),
        out_specs=(
            P(("section", "tp"), None),
            P(("section", "tp"), None),
            P(None, ("section", "tp"), None),
            P("section", None, "tp"),
            P("section", "tp", None),
        ),
        check_vma=False,
    )
```

profile of v0, /device:TPU:0, one launch (start us, length us, event | category | flops | bytes accessed | tf_op | source)
XLA Modules:
  0.0 429.3 jit_solution(4196626282191384859)
XLA Ops:
  7.2 2.9 copy.25
  12.6 5.9 %fusion.64 = (f32[6,384]{1,0:T(8,128)S(1)}, f32[6,384,384]{2,1,0:T(8,128)}) fusion(bf16[1,6,384,384]{3,2,1,0:T(8,128)(2,1)} %param.12, pred[384,384]{1,0:T(8,128)(4,1)S(1)} %iota_compare_fusion), kind=kOutput, calls=%fused_computation.81 | output fusion | flops 6193535 | bytes 5465088 | tf_op jit(solution)/shard_map/sub | solution.py:38
  18.5 2.2 fusion.65
  21.1 44.7 %all-gather.4.cloned.1.call-done = bf16[384,6144]{1,0:T(8,128)(2,1)} async-done(((bf16[48,6144]{1,0:T(8,128)(2,1)}), bf16[384,6144]{1,0:T(8,128)(2,1)}) %all-gather.4.cloned.1.call-update) | async-done | bytes 4718608 | tf_op jit(solution)/shard_map/all_gather | solution.py:67
  65.8 8.9 %fusion.38 = bf16[384,768]{1,0:T(8,128)(2,1)S(1)} fusion(bf16[384,6144]{1,0:T(8,128)(2,1)} %all-gather.4.cloned.1.call-done, bf16[1,6144,768]{2,1,0:T(8,128)(2,1)} %param.14), kind=kOutput, calls=%fused_computation.48 | convolution fusion | flops 3624173568 | bytes 14745600 | tf_op jit(solution)/shard_map/dot_general | solution.py:66
  75.0 2.8 fusion.37
  77.8 9.5 %fusion.17 = bf16[384,6144]{1,0:T(8,128)(2,1)} fusion(bf16[384,768]{0,1:T(8,128)(2,1)S(1)} %bitcast.100, bf16[1,768,6144]{2,1,0:T(8,128)(2,1)} %param.15), kind=kOutput, calls=%fused_computation.17 | convolution fusion | flops 3626237952 | bytes 14745600 | tf_op jit(solution)/shard_map/dot_general | solution.py:73
  87.3 30.2 %all-gather.6.cloned.1.call-done = bf16[384,6144]{1,0:T(8,128)(2,1)} async-done(((bf16[48,6144]{1,0:T(8,128)(2,1)}), bf16[384,6144]{1,0:T(8,128)(2,1)}) %all-gather.6.cloned.1.call-update) | async-done | bytes 4718608 | tf_op jit(solution)/shard_map/all_gather | solution.py:91
  117.4 9.0 %fusion.44 = bf16[384,768]{1,0:T(8,128)(2,1)S(1)} fusion(bf16[384,6144]{1,0:T(8,128)(2,1)} %all-gather.6.cloned.1.call-done, bf16[1,768,6144]{2,1,0:T(8,128)(2,1)} %param.15), kind=kOutput, calls=%fused_computation.50 | convolution fusion | flops 3624173568 | bytes 14745600 | tf_op jit(solution)/shard_map/td,hd->th/dot_general | solution.py:98
  128.1 14.5 %fusion.14 = bf16[384,6144]{1,0:T(8,128)(2,1)} fusion(bf16[384,768]{0,1:T(8,128)(2,1)S(1)} %bitcast.102, bf16[1,6144,768]{2,1,0:T(8,128)(2,1)} %param.14), kind=kOutput, calls=%fused_computation.16 | convolution fusion | flops 3626237952 | bytes 14745600 | tf_op jit(solution)/shard_map/th,dh->td/dot_general | solution.py:119
  148.6 26.8 %collective-permute-done.1 = bf16[2,48,6144]{2,1,0:T(8,128)(2,1)} collective-permute-done((bf16[2,48,6144]{2,1,0:T(8,128)(2,1)S(1)}, bf16[2,48,6144]{2,1,0:T(8,128)(2,1)}, u32[]{:S(2)}, u32[]{:S(2)}) %collective-permute-start.1) | collective-permute-done | bytes 1179680 | tf_op jit(solution)/shard_map/ppermute | solution.py:20
  176.8 26.0 %collective-permute-done.2 = bf16[2,48,6144]{2,1,0:T(8,128)(2,1)S(1)} collective-permute-done((bf16[2,48,6144]{2,1,0:T(8,128)(2,1)}, bf16[2,48,6144]{2,1,0:T(8,128)(2,1)S(1)}, u32[]{:S(2)}, u32[]{:S(2)}) %collective-permute-start.2) | collective-permute-done | bytes 1179680 | tf_op jit(solution)/shard_map/ppermute | solution.py:20
  203.4 133.5 %all-reduce.3.cloned.1.call-done = (bf16[384,6144]{1,0:T(8,128)(2,1)}, bf16[384,6144]{1,0:T(8,128)(2,1)}) async-done(((bf16[384,6144]{1,0:T(8,128)(2,1)}, bf16[384,6144]{1,0:T(8,128)(2,1)}), (bf16[384,6144]{1,0:T(8,128)(2,1)}, bf16[384,6144]{1,0:T(8,128)(2,1)})) %all-reduce.3.cloned.1.call-update) | async-done | bytes 9437200 | tf_op jit(solution)/shard_map/psum | solution.py:72
  336.9 1.5 convert_reduce_fusion
  338.4 2.7 fusion.52
  342.3 1.5 collective-permute-start
  343.9 1.5 collective-permute-start.3
  346.2 13.3 %collective-permute-done = bf16[48,6144]{1,0:T(8,128)(2,1)S(1)} collective-permute-done((bf16[48,6144]{1,0:T(8,128)(2,1)S(1)}, bf16[48,6144]{1,0:T(8,128)(2,1)S(1)}, u32[]{:S(2)}, u32[]{:S(2)}) %collective-permute-start) | collective-permute-done | bytes 589856 | tf_op jit(solution)/shard_map/ppermute | solution.py:14
  359.5 11.3 %collective-permute-done.3 = bf16[48,6144]{1,0:T(8,128)(2,1)} collective-permute-done((bf16[48,6144]{1,0:T(8,128)(2,1)}, bf16[48,6144]{1,0:T(8,128)(2,1)}, u32[]{:S(2)}, u32[]{:S(2)}) %collective-permute-start.3) | collective-permute-done | bytes 589856 | tf_op jit(solution)/shard_map/ppermute | solution.py:14
  370.8 21.8 %all-gather.8.cloned.1.call-done = bf16[384,6144]{1,0:T(8,128)(2,1)} async-done(((bf16[48,6144]{1,0:T(8,128)(2,1)}), bf16[384,6144]{1,0:T(8,128)(2,1)}) %all-gather.8.cloned.1.call-update) | async-done | bytes 4718608 | tf_op jit(solution)/shard_map/all_gather | solution.py:90
  392.6 8.9 %fusion.41 = bf16[384,768]{1,0:T(8,128)(2,1)S(1)} fusion(bf16[384,6144]{1,0:T(8,128)(2,1)} %all-gather.8.cloned.1.call-done, bf16[1,6144,768]{2,1,0:T(8,128)(2,1)} %param.14), kind=kOutput, calls=%fused_computation.49 | convolution fusion | flops 3624173568 | bytes 14745600 | tf_op jit(solution)/shard_map/dot_general | solution.py:94
  402.6 9.9 %fusion.12 = bf16[1,6144,768]{2,1,0:T(8,128)(2,1)} fusion(bf16[384,6144]{1,0:T(8,128)(2,1)} %all-gather.8.cloned.1.call-done, bf16[384,768]{0,1:T(8,128)(2,1)S(1)} %bitcast.103), kind=kOutput, calls=%fused_computation.14 | convolution fusion | flops 3628597248 | bytes 14745600 | tf_op jit(solution)/shard_map/td,th->dh/dot_general | solution.py:117
  412.5 7.4 %fusion.13 = bf16[1,768,6144]{2,1,0:T(8,128)(2,1)} fusion(bf16[384,768]{0,1:T(8,128)(2,1)S(1)} %bitcast.104, bf16[384,6144]{1,0:T(8,128)(2,1)S(1)} %bitcast.106), kind=kOutput, calls=%fused_computation.15 | convolution fusion | flops 3628597248 | bytes 14745600 | tf_op jit(solution)/shard_map/th,td->hd/dot_general | solution.py:105
  420.8 1.9 copy.27
  (52 shorter events, 14.7 us)
Async XLA Ops:
  7.2 2.9 copy-start
  7.2 58.6 %all-gather.4.cloned.1.call-start = ((), (), s32[]{:S(2)}) async-start(), calls=%async_computation | async-start | bytes 5308416 | tf_op jit(solution)/shard_map/all_gather | solution.py:67
  11.7 105.7 %all-gather.6.cloned.1.call-start = ((), (), s32[]{:S(2)}) async-start(), calls=%async_computation.1 | async-start | bytes 5308416 | tf_op jit(solution)/shard_map/all_gather | solution.py:91
  12.5 324.4 %all-reduce.3.cloned.1.call-start = ((), (), s32[]{:S(2)}) async-start(), calls=%async_computation.3 | async-start | bytes 18874368 | tf_op jit(solution)/shard_map/psum | solution.py:72
  12.6 5.9 %copy-start.5 = (bf16[1,6,384,384]{3,2,1,0:T(8,128)(2,1)S(1)}, bf16[1,6,384,384]{3,2,1,0:T(8,128)(2,1)}, u32[]{:S(2)}) copy-start(bf16[1,6,384,384]{3,2,1,0:T(8,128)(2,1)} %param.13) | copy-start | bytes 5308420
  127.3 0.8 copy-start.3
  142.6 0.7 copy-start.6
  142.6 250.0 %all-gather.8.cloned.1.call-start = ((), (), s32[]{:S(2)}) async-start(), calls=%async_computation.2 | async-start | bytes 5308416 | tf_op jit(solution)/shard_map/all_gather | solution.py:90
  147.1 28.2 %collective-permute-start.1 = (bf16[2,48,6144]{2,1,0:T(8,128)(2,1)S(1)}, bf16[2,48,6144]{2,1,0:T(8,128)(2,1)}, u32[]{:S(2)}, u32[]{:S(2)}) collective-permute-start(bf16[2,48,6144]{2,1,0:T(8,128)(2,1)S(1)} %pad_maximum_fusion), channel_id=1, source_target_pairs={{0,8},{8,0},{16,24},{24,16},{1,9},{9,1},{17,25},{25,17},{2,10},{10... | collective-permute-start | bytes 3538952 | tf_op jit(solution)/shard_map/ppermute | solution.py:20
  175.4 27.4 %collective-permute-start.2 = (bf16[2,48,6144]{2,1,0:T(8,128)(2,1)}, bf16[2,48,6144]{2,1,0:T(8,128)(2,1)S(1)}, u32[]{:S(2)}, u32[]{:S(2)}) collective-permute-start(bf16[2,48,6144]{2,1,0:T(8,128)(2,1)} %collective-permute-done.1), channel_id=1, source_target_pairs={{0,16},{8,24},{16,0},{24,8},{1,17},{9,25},{17,1},{25,9},{2,18},{10... | collective-permute-start | bytes 3538952 | tf_op jit(solution)/shard_map/ppermute | solution.py:20
  342.3 17.2 %collective-permute-start = (bf16[48,6144]{1,0:T(8,128)(2,1)S(1)}, bf16[48,6144]{1,0:T(8,128)(2,1)S(1)}, u32[]{:S(2)}, u32[]{:S(2)}) collective-permute-start(bf16[48,6144]{1,0:T(8,128)(2,1)S(1)} %fusion.59), channel_id=1, source_target_pairs={{0,8},{8,16},{16,24},{24,0},{1,9},{9,17},{17,25},{25,1},{2,10},{10... | collective-permute-start | bytes 1769480 | tf_op jit(solution)/shard_map/ppermute | solution.py:14
  343.9 26.9 %collective-permute-start.3 = (bf16[48,6144]{1,0:T(8,128)(2,1)}, bf16[48,6144]{1,0:T(8,128)(2,1)}, u32[]{:S(2)}, u32[]{:S(2)}) collective-permute-start(bf16[48,6144]{1,0:T(8,128)(2,1)} %get-tuple-element.10), channel_id=1, source_target_pairs={{0,24},{8,0},{16,8},{24,16},{1,25},{9,1},{17,9},{25,17},{2,26},{10... | collective-permute-start | bytes 1769480 | tf_op jit(solution)/shard_map/ppermute | solution.py:14
  359.5 33.1 %copy-start.1 = (bf16[48,6144]{1,0:T(8,128)(2,1)}, bf16[48,6144]{1,0:T(8,128)(2,1)S(1)}, u32[]{:S(2)}) copy-start(bf16[48,6144]{1,0:T(8,128)(2,1)S(1)} %collective-permute-done) | copy-start | bytes 1769476
  401.6 1.1 copy-start.4
  401.9 10.7 %slice-start = ((s8[4718592]{0:T(1024)(128)(4,1)}), s8[4194304]{0:T(1024)(128)(4,1)S(1)}, s32[]{:S(2)}) async-start(s8[4718592]{0:T(1024)(128)(4,1)} %bitcast.105), calls=%async_computation.4 | async-start | bytes 8388608
  402.6 9.9 %slice-start.1 = ((s8[4718592]{0:T(1024)(128)(4,1)}), s8[524288]{0:T(1024)(128)(4,1)S(1)}, s32[]{:S(2)}) async-start(s8[4718592]{0:T(1024)(128)(4,1)} %bitcast.105), calls=%async_computation.5 | async-start | bytes 1048576
  412.5 7.5 %copy-start.2 = (bf16[48,6144]{1,0:T(8,128)(2,1)S(1)}, bf16[48,6144]{1,0:T(8,128)(2,1)}, u32[]{:S(2)}) copy-start(bf16[48,6144]{1,0:T(8,128)(2,1)} %copy-done.1) | copy-start | bytes 1769476
Sparse Core Ops, SparseCore 0:
  11.8 53.9 all-gather.3
  67.4 49.9 all-gather.5
  142.7 194.0 all-reduce.2
  341.3 51.3 all-gather.7
where the time goes:
time: 430 us; the launch traced here: 429 us
  waiting for transfers between devices  308 us (72%)
  matrix products  72.1 us (17%)
  other arithmetic  16.9 us (4%)
  between operations  15.9 us (4%)
  local copies, waits for them, and re-layouts  10.1 us (2%)
  starting transfers between devices  5.99 us (1%)
    psum x1, waiting for transfers between devices, per_device(): lax.psum(jnp.dot(context, weight_out, preferred_element_type=jnp.float32)...  134 us
    ppermute x2, waiting for transfers between devices, partner(): return lax.ppermute(value, axis, pairs)  52.8 us
    all_gather x1, waiting for transfers between devices, per_device(): lax.all_gather(normed, 'tp', axis=0, tiled=True)  44.7 us
    all_gather x1, waiting for transfers between devices, per_device(): piece_cot = lax.all_gather(cotangents, 'tp', axis=0, tiled=True)  30.2 us
    ppermute x2, waiting for transfers between devices, passed_along(): lax.ppermute(array, axis, [(i, (i + by) % size) for i in range(size)])  24.6 us
    all_gather x1, waiting for transfers between devices, per_device(): piece_norm = lax.all_gather(stash_normed, 'tp', axis=0, tiled=True)  21.8 us
    dot_general x1, matrix products, per_device(): jnp.einsum('th,dh->td', value_back, weight_in, preferred_element_type=jnp...  14.5 us
    dot_general x1, matrix products, per_device(): jnp.einsum('td,th->dh', rows_norm, value_back, preferred_element_type=jnp...  9.91 us
  transfers between devices with their start and end apart: 8, of which 8 were waited for; matrix products, arithmetic and copies ran while one was open for 8% of the time, Pallas kernels for 0%

commit v1 on v0

v1 whole, which is shorter than its diff:
```python
import jax
import jax.numpy as jnp
from jax import lax
from jax.sharding import PartitionSpec as P


HEAD = 128


eps = 1e-05


def passed_along(array, axis, by):
    size = lax.axis_size(axis)
    return lax.ppermute(array, axis, [(i, (i + by) % size) for i in range(size)])


def normalize(layer_rows):
    average = jnp.mean(layer_rows, axis=-1, keepdims=True)
    centred = layer_rows - average
    inv_scale = lax.rsqrt(jnp.mean(centred * centred, axis=-1, keepdims=True) + eps)
    return (centred * inv_scale, inv_scale)


def causal_softmax(scores):
    logits = scores.astype(jnp.float32)
    rows = logits.shape[-1]
    causal = lax.broadcasted_iota(jnp.int32, (rows, rows), 0) >= lax.broadcasted_iota(
        jnp.int32, (rows, rows), 1
    )
    logits = jnp.where(causal, logits, -1e30)
    row_top = jnp.max(logits, axis=-1, keepdims=True)
    raised = jnp.where(causal, jnp.exp(logits - row_top), 0.0)
    return (raised / jnp.sum(raised, axis=-1, keepdims=True)).astype(jnp.bfloat16)


def mix_heads(weights, value_rows):
    rows = value_rows.shape[0]
    head_count = weights.shape[0]
    by_head = value_rows.reshape(rows, head_count, HEAD)
    mixed = jnp.einsum("hqk,khe->qhe", weights, by_head, preferred_element_type=jnp.float32)
    return mixed.reshape(rows, head_count * HEAD).astype(jnp.bfloat16)


def reduce_rows(partial):
    return lax.psum_scatter(
        partial.astype(jnp.bfloat16), "tp", scatter_dimension=0, tiled=True
    ).astype(jnp.float32)


def mirrored(array):
    size = lax.axis_size("section")
    return lax.ppermute(array, "section", [(i, size - 1 - i) for i in range(size)])


def per_device(
    inputs_now, cotangents, stashed, plan, fwd_scores, back_scores, value_weight, out_weight
):
    tp_count = lax.axis_size("tp")
    sections = lax.axis_size("section")
    section_idx = lax.axis_index("section")
    mirror = sections - 1 - section_idx
    share_rows = inputs_now.shape[0]
    all_rows = share_rows * tp_count
    weight_in = value_weight[0]
    weight_out = out_weight[0]
    col_share = weight_in.shape[1]
    head_count = back_scores.shape[1]

    rows_cot = lax.all_gather(cotangents, "tp", axis=0, tiled=True)
    lookup = jnp.arange(sections, dtype=jnp.int32)
    owner_slot = jnp.sum(jnp.where(lookup == mirror, plan, 0))
    guest_rows = lax.dynamic_index_in_dim(stashed, owner_slot, 0, keepdims=False)
    stored = mirrored(guest_rows)
    arrived = mirrored(inputs_now)
    layer_rows = inputs_now.astype(jnp.float32)
    unit_rows, _ = normalize(layer_rows)
    normed = unit_rows.astype(jnp.bfloat16)
    rows_now = lax.all_gather(normed, "tp", axis=0, tiled=True)

    back_probs = causal_softmax(back_scores[0])
    fwd_probs = causal_softmax(fwd_scores[0])

    rows_grad = jnp.einsum(
        "td,hd->th", rows_cot, weight_out, preferred_element_type=jnp.float32
    ).astype(jnp.bfloat16)
    value_back = (
        jnp.einsum(
            "hqk,qhe->khe",
            back_probs,
            rows_grad.reshape(all_rows, head_count, HEAD),
            preferred_element_type=jnp.float32,
        )
        .reshape(all_rows, col_share)
        .astype(jnp.bfloat16)
    )
    partial_back = jnp.einsum(
        "th,dh->td", value_back, weight_in, preferred_element_type=jnp.float32
    )
    norm_grad = reduce_rows(partial_back)

    stash_unit, stash_scale = normalize(stored.astype(jnp.float32))
    stash_normed = stash_unit.astype(jnp.bfloat16)
    rows_norm = lax.all_gather(stash_normed, "tp", axis=0, tiled=True)

    rows_now, stash_normed = lax.optimization_barrier((rows_now, stash_normed))
    values = jnp.dot(rows_now, weight_in, preferred_element_type=jnp.float32).astype(jnp.bfloat16)
    context = mix_heads(fwd_probs, values)
    partial = jnp.dot(context, weight_out, preferred_element_type=jnp.float32)
    branch = reduce_rows(partial)

    input_grad = cotangents.astype(jnp.float32) + stash_scale * (
        norm_grad
        - jnp.mean(norm_grad, axis=-1, keepdims=True)
        - stash_unit * jnp.mean(norm_grad * stash_unit, axis=-1, keepdims=True)
    )
    grad_back = passed_along(input_grad.astype(jnp.bfloat16), "section", -1)

    rows_value = jnp.dot(rows_norm, weight_in, preferred_element_type=jnp.float32).astype(
        jnp.bfloat16
    )
    stash_context = mix_heads(back_probs, rows_value)
    grad_outw = jnp.einsum("th,td->hd", stash_context, rows_cot, preferred_element_type=jnp.float32)
    grad_valw = jnp.einsum("td,th->dh", rows_norm, value_back, preferred_element_type=jnp.float32)
    stash_next = lax.dynamic_update_index_in_dim(stashed, arrived, owner_slot, 0)

    layer_out = (layer_rows + branch).astype(jnp.bfloat16)
    handed_on = passed_along(layer_out, "section", 1)
    return (
        handed_on,
        grad_back,
        stash_next,
        grad_valw.astype(jnp.bfloat16)[None],
        grad_outw.astype(jnp.bfloat16)[None],
    )


def solution(mesh):
    return jax.shard_map(
        per_device,
        mesh=mesh,
        in_specs=(
            P(("section", "tp"), None),
            P(("section", "tp"), None),
            P(None, ("section", "tp"), None),
            P(),
            P("section", "tp", None, None),
            P("section", "tp", None, None),
            P("section", None, "tp"),
            P("section", "tp", None),
        ),
        out_specs=(
            P(("section", "tp"), None),
            P(("section", "tp"), None),
            P(None, ("section", "tp"), None),
            P("section", None, "tp"),
            P("section", "tp", None),
        ),
        check_vma=False,
    )
```

time: 430 us -> 328 us (0.76)
  waiting for transfers between devices: 308 us -> 197 us
    psum x1 -> x0, waiting for transfers between devices: 134 us -> none  [per_device(): lax.psum(jnp.dot(context, weight_out, preferred_element_type=jnp.float32)...]
    reduce_scatter x0 -> x2, waiting for transfers between devices: none -> 51.5 us  [reduce_rows(): lax.psum_scatter(partial.astype(jnp.bfloat16), 'tp', scatter_dimension=0,...]
    ppermute x2, waiting for transfers between devices: 52.8 us -> 24.6 us  [mirrored(): lax.ppermute(array, 'section', [(i, size - 1 - i) for i in range(size)])]
    ppermute x2, waiting for transfers between devices: 24.6 us -> 15.8 us  [passed_along(): lax.ppermute(array, axis, [(i, (i + by) % size) for i in range(size)])]
    all_gather x3, waiting for transfers between devices: 96.7 us -> 105 us  [the longest x1 49.4 us: per_device(): rows_cot = lax.all_gather(cotangents, 'tp', axis=0, tiled=True)]
  transfers between devices with their start and end apart: 8 -> 9, of which waited for: 8 -> 9; matrix products, arithmetic and copies ran while one was open for 8% -> 22% of each run, Pallas kernels for 0% -> 0%
where the time goes in v1:
time: 328 us
  waiting for transfers between devices  197 us (60%)
  matrix products  75.4 us (23%)
  other arithmetic  18.5 us (6%)
  between operations  15.8 us (5%)
  local copies, waits for them, and re-layouts  11.2 us (3%)
  starting transfers between devices  9.36 us (3%)
    reduce_scatter x2, waiting for transfers between devices, reduce_rows(): lax.psum_scatter(partial.astype(jnp.bfloat16), 'tp', scatter_dimension=0,...  51.5 us
    all_gather x1, waiting for transfers between devices, per_device(): rows_cot = lax.all_gather(cotangents, 'tp', axis=0, tiled=True)  49.4 us
    all_gather x1, waiting for transfers between devices, per_device(): rows_now = lax.all_gather(normed, 'tp', axis=0, tiled=True)  41.7 us
    ppermute x2, waiting for transfers between devices, mirrored(): lax.ppermute(array, 'section', [(i, size - 1 - i) for i in range(size)])  24.6 us
    ppermute x2, waiting for transfers between devices, passed_along(): lax.ppermute(array, axis, [(i, (i + by) % size) for i in range(size)])  15.8 us
    dot_general x1, matrix products, per_device(): jnp.einsum('th,dh->td', value_back, weight_in, preferred_element_type=jnp...  14.5 us
    all_gather x1, waiting for transfers between devices, per_device(): rows_norm = lax.all_gather(stash_normed, 'tp', axis=0, tiled=True)  14.1 us
    sub x2, other arithmetic, causal_softmax(): raised = jnp.where(causal, jnp.exp(logits - row_top), 0.0)  10 us
  transfers between devices with their start and end apart: 9, of which 9 were waited for; matrix products, arithmetic and copies ran while one was open for 22% of the time, Pallas kernels for 0%

profile of v1, /device:TPU:0, one launch (start us, length us, event | category | flops | bytes accessed | tf_op | source)
XLA Modules:
  0.0 327.6 jit_solution(8753069891616576866)
XLA Ops:
  7.2 2.8 copy.23
  10.2 4.2 %fusion.63 = (f32[6,384]{1,0:T(8,128)S(1)}, f32[6,384,384]{2,1,0:T(8,128)S(1)}) fusion(bf16[1,6,384,384]{3,2,1,0:T(8,128)(2,1)} %param.13, pred[384,384]{1,0:T(8,128)(4,1)S(1)} %iota_compare_fusion), kind=kOutput, calls=%fused_computation.79 | output fusion | flops 6193535 | bytes 5465088 | tf_op jit(solution)/shard_map/sub | solution.py:33
  14.8 49.4 %all-gather.6.cloned.1.call-done = bf16[384,6144]{1,0:T(8,128)(2,1)} async-done(((bf16[48,6144]{1,0:T(8,128)(2,1)}), bf16[384,6144]{1,0:T(8,128)(2,1)}) %all-gather.6.cloned.1.call-update) | async-done | bytes 4718608 | tf_op jit(solution)/shard_map/all_gather | solution.py:70
  64.2 9.0 %fusion.48 = bf16[384,768]{1,0:T(8,128)(2,1)S(1)} fusion(bf16[384,6144]{1,0:T(8,128)(2,1)} %all-gather.6.cloned.1.call-done, bf16[1,768,6144]{2,1,0:T(8,128)(2,1)} %param.15), kind=kOutput, calls=%fused_computation.54 | convolution fusion | flops 3624173568 | bytes 14745600 | tf_op jit(solution)/shard_map/td,hd->th/dot_general | solution.py:84
  74.8 14.5 %fusion.14 = bf16[384,6144]{1,0:T(8,128)(2,1)} fusion(bf16[384,768]{0,1:T(8,128)(2,1)S(1)} %bitcast.78, bf16[1,6144,768]{2,1,0:T(8,128)(2,1)} %param.14), kind=kOutput, calls=%fused_computation.16 | convolution fusion | flops 3626237952 | bytes 14745600 | tf_op jit(solution)/shard_map/th,dh->td/dot_general | solution.py:97
  92.0 2.4 collective-permute-start.3
  97.0 11.4 %collective-permute-done.3 = bf16[48,6144]{1,0:T(8,128)(2,1)S(1)} collective-permute-done((bf16[48,6144]{1,0:T(8,128)(2,1)S(1)}, bf16[48,6144]{1,0:T(8,128)(2,1)S(1)}, u32[]{:S(2)}, u32[]{:S(2)}) %collective-permute-start.3) | collective-permute-done | bytes 589856 | tf_op jit(solution)/shard_map/ppermute | solution.py:53
  110.4 2.4 collective-permute-start
  112.8 13.2 %collective-permute-done = bf16[48,6144]{1,0:T(8,128)(2,1)S(1)} collective-permute-done((bf16[48,6144]{1,0:T(8,128)(2,1)S(1)}, bf16[48,6144]{1,0:T(8,128)(2,1)S(1)}, u32[]{:S(2)}, u32[]{:S(2)}) %collective-permute-start) | collective-permute-done | bytes 589856 | tf_op jit(solution)/shard_map/ppermute | solution.py:53
  126.6 16.5 %reduce-scatter.5.cloned.1.call-done = bf16[48,6144]{1,0:T(8,128)(2,1)} async-done(((bf16[384,6144]{1,0:T(8,128)(2,1)}), bf16[48,6144]{1,0:T(8,128)(2,1)}) %reduce-scatter.5.cloned.1.call-update) | async-done | bytes 589840 | tf_op jit(solution)/shard_map/reduce_scatter | solution.py:46
  144.6 2.6 fusion.56
  147.4 5.9 %fusion.64 = (f32[6,384]{1,0:T(8,128)S(1)}, f32[6,384,384]{2,1,0:T(8,128)}) fusion(bf16[1,6,384,384]{3,2,1,0:T(8,128)(2,1)} %param.12, pred[384,384]{1,0:T(8,128)(4,1)} %copy-done.5), kind=kOutput, calls=%fused_computation.80 | output fusion | flops 6193535 | bytes 5465088 | tf_op jit(solution)/shard_map/sub | solution.py:33
  153.3 41.7 %all-gather.4.cloned.1.call-done = bf16[384,6144]{1,0:T(8,128)(2,1)} async-done(((bf16[48,6144]{1,0:T(8,128)(2,1)}), bf16[384,6144]{1,0:T(8,128)(2,1)}) %all-gather.4.cloned.1.call-update) | async-done | bytes 4718608 | tf_op jit(solution)/shard_map/all_gather | solution.py:79
  195.0 8.9 %fusion.42 = bf16[384,768]{1,0:T(8,128)(2,1)S(1)} fusion(bf16[384,6144]{1,0:T(8,128)(2,1)} %all-gather.4.cloned.1.call-done, bf16[1,6144,768]{2,1,0:T(8,128)(2,1)} %param.14), kind=kOutput, calls=%fused_computation.52 | convolution fusion | flops 3624173568 | bytes 14745600 | tf_op jit(solution)/shard_map/dot_general | solution.py:107
  204.3 2.8 fusion.41
  207.1 9.3 %fusion.17 = bf16[384,6144]{1,0:T(8,128)(2,1)} fusion(bf16[384,768]{0,1:T(8,128)(2,1)S(1)} %bitcast.76, bf16[1,768,6144]{2,1,0:T(8,128)(2,1)} %param.15), kind=kOutput, calls=%fused_computation.17 | convolution fusion | flops 3626237952 | bytes 14745600 | tf_op jit(solution)/shard_map/dot_general | solution.py:109
  217.4 2.6 collective-permute-start.2
  220.1 12.9 %collective-permute-done.2 = bf16[48,6144]{1,0:T(8,128)(2,1)S(1)} collective-permute-done((bf16[48,6144]{1,0:T(8,128)(2,1)S(1)}, bf16[48,6144]{1,0:T(8,128)(2,1)S(1)}, u32[]{:S(2)}, u32[]{:S(2)}) %collective-permute-start.2) | collective-permute-done | bytes 589856 | tf_op jit(solution)/shard_map/ppermute | solution.py:15
  233.0 14.1 %all-gather.8.cloned.1.call-done = bf16[384,6144]{1,0:T(8,128)(2,1)} async-done(((bf16[48,6144]{1,0:T(8,128)(2,1)}), bf16[384,6144]{1,0:T(8,128)(2,1)}) %all-gather.8.cloned.1.call-update) | async-done | bytes 4718608 | tf_op jit(solution)/shard_map/all_gather | solution.py:104
  247.1 9.7 %fusion.45 = bf16[384,768]{1,0:T(8,128)(2,1)} fusion(bf16[384,6144]{1,0:T(8,128)(2,1)} %all-gather.8.cloned.1.call-done, bf16[1,6144,768]{2,1,0:T(8,128)(2,1)} %param.14), kind=kOutput, calls=%fused_computation.53 | convolution fusion | flops 3624173568 | bytes 14745600 | tf_op jit(solution)/shard_map/dot_general | solution.py:119
  259.7 9.4 %fusion.12 = bf16[1,6144,768]{2,1,0:T(8,128)(2,1)} fusion(bf16[384,6144]{1,0:T(8,128)(2,1)} %all-gather.8.cloned.1.call-done, bf16[384,768]{0,1:T(8,128)(2,1)} %bitcast.79), kind=kOutput, calls=%fused_computation.14 | convolution fusion | flops 3628597248 | bytes 14745600 | tf_op jit(solution)/shard_map/td,th->dh/dot_general | solution.py:124
  269.1 35.0 %reduce-scatter.3.cloned.1.call-done = bf16[48,6144]{1,0:T(8,128)(2,1)} async-done(((bf16[384,6144]{1,0:T(8,128)(2,1)}), bf16[48,6144]{1,0:T(8,128)(2,1)}) %reduce-scatter.3.cloned.1.call-update) | async-done | bytes 589840 | tf_op jit(solution)/shard_map/reduce_scatter | solution.py:46
  306.8 9.8 %fusion.13 = bf16[1,768,6144]{2,1,0:T(8,128)(2,1)} fusion(bf16[384,768]{0,1:T(8,128)(2,1)S(1)} %bitcast.80, bf16[384,6144]{1,0:T(8,128)(2,1)} %all-gather.6.cloned.1.call-done), kind=kOutput, calls=%fused_computation.15 | convolution fusion | flops 3628597248 | bytes 14745600 | tf_op jit(solution)/shard_map/th,td->hd/dot_general | solution.py:123
  316.5 2.9 collective-permute-done.1
  (48 shorter events, 18.3 us)
Async XLA Ops:
  7.2 57.0 %all-gather.6.cloned.1.call-start = ((), (), s32[]{:S(2)}) async-start(), calls=%async_computation.4 | async-start | bytes 5308416 | tf_op jit(solution)/shard_map/all_gather | solution.py:70
  10.1 133.0 %reduce-scatter.5.cloned.1.call-start = ((), (), s32[]{:S(2)}) async-start(), calls=%async_computation.5 | async-start | bytes 5308416 | tf_op jit(solution)/shard_map/reduce_scatter | solution.py:46
  10.2 4.2 %copy-start.5 = (pred[384,384]{1,0:T(8,128)(4,1)}, pred[384,384]{1,0:T(8,128)(4,1)S(1)}, u32[]{:S(2)}) copy-start(pred[384,384]{1,0:T(8,128)(4,1)S(1)} %iota_compare_fusion) | copy-start | bytes 442372
  74.0 0.8 copy-start.3
  89.3 1.1 copy-start
  89.3 5.2 %copy-start.6 = (s32[4]{0:T(128)S(1)}, s32[4]{0:T(128)}, u32[]{:S(2)}) copy-start(s32[4]{0:T(128)} %param.11) | copy-start | bytes 52
  89.3 105.7 %all-gather.4.cloned.1.call-start = ((), (), s32[]{:S(2)}) async-start(), calls=%async_computation.2 | async-start | bytes 5308416 | tf_op jit(solution)/shard_map/all_gather | solution.py:79
  90.6 54.0 %copy-start.1 = (bf16[48,6144]{1,0:T(8,128)(2,1)S(1)}, bf16[48,6144]{1,0:T(8,128)(2,1)}, u32[]{:S(2)}) copy-start(bf16[48,6144]{1,0:T(8,128)(2,1)} %param.9) | copy-start | bytes 1769476
  92.0 155.1 %all-gather.8.cloned.1.call-start = ((), (), s32[]{:S(2)}) async-start(), calls=%async_computation.6 | async-start | bytes 5308416 | tf_op jit(solution)/shard_map/all_gather | solution.py:104
  92.0 16.4 %collective-permute-start.3 = (bf16[48,6144]{1,0:T(8,128)(2,1)S(1)}, bf16[48,6144]{1,0:T(8,128)(2,1)S(1)}, u32[]{:S(2)}, u32[]{:S(2)}) collective-permute-start(bf16[48,6144]{1,0:T(8,128)(2,1)S(1)} %copy-done), channel_id=1, source_target_pairs={{0,24},{8,16},{16,8},{24,0},{1,25},{9,17},{17,9},{25,1},{2,26},{10... | collective-permute-start | bytes 1769480 | tf_op jit(solution)/shard_map/ppermute | solution.py:53
  110.4 15.6 %collective-permute-start = (bf16[48,6144]{1,0:T(8,128)(2,1)S(1)}, bf16[48,6144]{1,0:T(8,128)(2,1)S(1)}, u32[]{:S(2)}, u32[]{:S(2)}) collective-permute-start(bf16[48,6144]{1,0:T(8,128)(2,1)S(1)} %get-tuple-element.10), channel_id=1, source_target_pairs={{0,24},{8,16},{16,8},{24,0},{1,25},{9,17},{17,9},{25,1},{2,26},{10... | collective-permute-start | bytes 1769480 | tf_op jit(solution)/shard_map/ppermute | solution.py:53
  147.2 156.9 %reduce-scatter.3.cloned.1.call-start = ((), (), s32[]{:S(2)}) async-start(), calls=%async_computation.3 | async-start | bytes 5308416 | tf_op jit(solution)/shard_map/reduce_scatter | solution.py:46
  216.4 1.1 copy-start.2
  217.4 15.5 %collective-permute-start.2 = (bf16[48,6144]{1,0:T(8,128)(2,1)S(1)}, bf16[48,6144]{1,0:T(8,128)(2,1)S(1)}, u32[]{:S(2)}, u32[]{:S(2)}) collective-permute-start(bf16[48,6144]{1,0:T(8,128)(2,1)S(1)} %copy-done.2), channel_id=1, source_target_pairs={{0,24},{8,0},{16,8},{24,16},{1,25},{9,1},{17,9},{25,17},{2,26},{10... | collective-permute-start | bytes 1769480 | tf_op jit(solution)/shard_map/ppermute | solution.py:15
  259.7 47.1 %copy-start.4 = (bf16[6,128,384]{2,1,0:T(8,128)(2,1)S(1)}, bf16[6,128,384]{2,1,0:T(8,128)(2,1)}, u32[]{:S(2)}) copy-start(bf16[6,128,384]{2,1,0:T(8,128)(2,1)} %convolution_convert_fusion.2) | copy-start | bytes 1769476
  305.2 14.1 %collective-permute-start.1 = (bf16[48,6144]{1,0:T(8,128)(2,1)S(1)}, bf16[48,6144]{1,0:T(8,128)(2,1)S(1)}, u32[]{:S(2)}, u32[]{:S(2)}) collective-permute-start(bf16[48,6144]{1,0:T(8,128)(2,1)S(1)} %fusion.58), channel_id=1, source_target_pairs={{0,8},{8,16},{16,24},{24,0},{1,9},{9,17},{17,25},{25,1},{2,10},{10... | collective-permute-start | bytes 1769480 | tf_op jit(solution)/shard_map/ppermute | solution.py:15
Sparse Core Ops, SparseCore 0:
  10.2 53.9 all-gather.5
  89.4 53.6 reduce-scatter.4
  145.3 49.6 all-gather.3
  197.1 49.9 all-gather.7
  249.8 54.1 reduce-scatter.2
